TPU v7x, 32 devices: a whole 2x2x4 slice. The times are simulated.
32 devices in a mesh: fx: 8 (over z, x), fy: 4 (over y, core).
Axes of the slice: x: 2, y: 2, z: 4, core: 2. Of those that a mesh axis runs over, the one named last changes fastest.
Arguments:
- right_side: float32 [512, 2048], P(('fx', 'fy'))
- coupling: float32 [512, 11, 4096], P(('fx', 'fy')), may hold values from -0.109375 to 0.109375
- face_columns: int32 [512, 11], P(('fx', 'fy')), may hold values from 0 to 31, as said below
- ghost_lists: int32 [128, 4], P(('fx', 'fy')), may hold values from 0 to 15, as said below
Outputs:
- solution: float32 [512, 2048], P(('fx', 'fy'))
- residual: float32 [512, 2048], P(('fx', 'fy'))
Inputs may be any that keep to these rules, and one draw needn't show every extreme that they name: face_columns[f, 0] is f's own index within its block; entries 1 to 6 name other faces of the same block, all distinct and below 16; entries 7 to 10 are distinct and name received faces, 16 + d * 4 + g for the g-th face of group d of the extended list; every received slot of every block is named by some row of that block. `ghost_lists`: each row names 4 distinct faces of its block by local index.
All inputs are finite; a program needn't handle non-finite values.
Results may differ from a plain program's by a relative error of at most 0.0003.
Values sent between devices are 32-bit elements; how exact they have to be, the bound alone decides.
A program may use at most 64 MiB of HBM per device.

v0:
```python
import jax
import jax.numpy as jnp
from jax import lax
from jax.sharding import PartitionSpec as P

DOF = 64
NRHS = 32
BLOCKS = 11
POWERS = 3


def from_behind(block, axis, distance):
    devices = range(lax.axis_size(axis))
    route = [(i - distance, i) for i in devices if i - distance in devices]
    return lax.ppermute(block, axis, route)


def receive_rows(field, ghost_lists):
    from_lower_x = from_behind(jnp.take(field, ghost_lists[1], axis=0), "fx", 1)
    from_upper_x = from_behind(jnp.take(field, ghost_lists[0], axis=0), "fx", -1)
    from_lower_y = from_behind(jnp.take(field, ghost_lists[3], axis=0), "fy", 1)
    from_upper_y = from_behind(jnp.take(field, ghost_lists[2], axis=0), "fy", -1)
    return jnp.concatenate([from_lower_x, from_upper_x, from_lower_y, from_upper_y], axis=0)


def contract(block_mats, picked):
    face_count = picked.shape[0]
    shaped = picked.reshape(face_count, picked.shape[1], DOF, NRHS)
    result = jnp.einsum("fkab,fkbr->far", block_mats, shaped, precision=lax.Precision.HIGHEST)
    return result.reshape(face_count, DOF * NRHS)


def solve_small(gram_total):
    count = NRHS
    row_ids = jnp.arange((POWERS + 1) * count)[:, None]
    col_ids = jnp.arange(POWERS * count)[None, :]
    shift_map = ((row_ids == col_ids) | (row_ids == col_ids + count)).astype(jnp.float32)
    first = (row_ids == jnp.arange(count)[None, :]).astype(jnp.float32)
    high = lax.Precision.HIGHEST
    normal_matrix = jnp.dot(
        shift_map.T, jnp.dot(gram_total, shift_map, precision=high), precision=high
    )
    right_terms = jnp.dot(shift_map.T, gram_total[:, :count], precision=high)
    factor = jnp.linalg.cholesky(normal_matrix)
    coeffs = jax.scipy.linalg.cho_solve((factor, True), right_terms)
    combo = first - jnp.dot(shift_map, coeffs, precision=high)
    return (coeffs, combo)


def on_device(right_side, coupling, face_columns, ghost_lists):
    face_count = right_side.shape[0]
    block_mats = coupling.reshape(face_count, BLOCKS, DOF, DOF)
    high = lax.Precision.HIGHEST

    def as_rows(field):
        return field.reshape(face_count * DOF, NRHS)

    fields = [right_side]
    partial_grams = []
    for power_index in range(POWERS + 1):
        if power_index > 0:
            power_field = fields[-1]
            received = receive_rows(power_field, ghost_lists)
            extended = jnp.concatenate([power_field, received], axis=0)
            fields.append(contract(block_mats, jnp.take(extended, face_columns, axis=0)))
        earlier_rows = jnp.concatenate([as_rows(item) for item in fields], axis=1)
        local_block = jnp.dot(
            earlier_rows.T, as_rows(fields[-1]), precision=high, preferred_element_type=jnp.float32
        )
        partial_grams.append(lax.psum(local_block, ("fx", "fy")))
    total_cols = (POWERS + 1) * NRHS
    upper_part = jnp.concatenate(
        [
            jnp.concatenate(
                [item, jnp.zeros((total_cols - item.shape[0], NRHS), jnp.float32)], axis=0
            )
            for item in partial_grams
        ],
        axis=1,
    )
    block_index = jnp.arange(total_cols) // NRHS
    gram_total = jnp.where(block_index[:, None] <= block_index[None, :], upper_part, upper_part.T)
    stacked = jnp.concatenate([as_rows(item) for item in fields], axis=1)
    coeffs, combo = solve_small(gram_total)
    solution = jnp.dot(stacked[:, : POWERS * NRHS], coeffs, precision=high)
    residual = jnp.dot(stacked, combo, precision=high)
    return (solution.reshape(face_count, DOF * NRHS), residual.reshape(face_count, DOF * NRHS))


def solution(mesh):
    placed = (
        P(("fx", "fy"), None),
        P(("fx", "fy"), None, None),
        P(("fx", "fy"), None),
        P(("fx", "fy"), None),
    )
    return jax.shard_map(
        on_device,
        mesh=mesh,
        in_specs=placed,
        out_specs=(P(("fx", "fy"), None), P(("fx", "fy"), None)),
        check_vma=False,
    )
```

profile of v0, /device:TPU:0, one launch (start us, length us, event | category | flops | bytes accessed | tf_op | source)
XLA Modules:
  0.0 199.0 jit_solution(18109654426102840548)
XLA Ops:
  0.6 0.8 compare_and_fusion.1
  1.5 1.5 gather_fusion
  3.1 4.9 %collective-permute-start = (f32[4,2048]{1,0:T(4,128)S(1)}, f32[4,2048]{1,0:T(4,128)S(1)}, u32[]{:S(2)}, u32[]{:S(2)}) collective-permute-start(f32[4,2048]{1,0:T(4,128)S(1)} %broadcast_select_fusion.14), channel_id=1, source_target_pairs={{0,4},{4,8},{8,12},{12,16},{16,20},{20,24},{24,28},{1,5},{5,9},{9,... | collective-permute-start | bytes 98312 | tf_op jit(solution)/shard_map/ppermute | solution.py:15
  7.9 1.5 gather_fusion.1
  9.5 1.3 collective-permute-start.1
  10.8 1.5 gather_fusion.2
  12.4 1.4 collective-permute-start.2
  13.9 1.5 gather_fusion.3
  15.4 1.3 collective-permute-start.3
  16.7 0.7 compare_select_fusion
  17.4 0.7 compare_and_fusion
  18.1 1.1 reshape.90
  19.3 1.0 fusion.40
  20.3 5.7 %reshape.92 = f32[16,11,64,64]{3,2,0,1:T(8,128)} reshape(f32[16,11,4096]{2,0,1:T(8,128)} %param.9) | data formatting | bytes 5767168 | tf_op jit(solution)/shard_map/reshape | solution.py:52
  26.2 1.2 gather_fusion.4
  27.3 1.5 reshape.248
  28.9 1.8 broadcast_select_fusion.2
  30.7 3.6 %reshape.276 = f32[16,11,64,32]{3,2,1,0:T(8,128)} reshape(f32[16,11,2048]{2,1,0:T(8,128)S(1)} %broadcast_select_fusion.2) | data formatting | bytes 2883584 | tf_op jit(solution)/shard_map/reshape | solution.py:28
  34.2 12.0 %fusion.6 = f32[16,64,32]{1,2,0:T(8,128)S(1)} fusion(f32[16,11,64,64]{3,2,0,1:T(8,128)} %reshape.92, f32[16,11,64,32]{3,2,1,0:T(8,128)} %reshape.276), kind=kOutput, calls=%fused_computation.21 | convolution fusion | flops 276824064 | bytes 4456448 | tf_op jit(solution)/shard_map/fkab,fkbr->far/dot_general | solution.py:29
  49.3 1.3 collective-permute-start.5
  50.6 4.6 %collective-permute-start.6 = (f32[4,2048]{1,0:T(4,128)S(1)}, f32[4,2048]{1,0:T(4,128)S(1)}, u32[]{:S(2)}, u32[]{:S(2)}) collective-permute-start(f32[4,2048]{1,0:T(4,128)S(1)} %broadcast_select_fusion.8), channel_id=1, source_target_pairs={{0,1},{1,2},{2,3},{4,5},{5,6},{6,7},{8,9},{9,10},{10,11},{12,13},{... | collective-permute-start | bytes 98312 | tf_op jit(solution)/shard_map/ppermute | solution.py:15
  55.3 1.3 collective-permute-start.7
  56.7 5.3 %collective-permute-start.4 = (f32[4,2048]{1,0:T(4,128)S(1)}, f32[4,2048]{1,0:T(4,128)S(1)}, u32[]{:S(2)}, u32[]{:S(2)}) collective-permute-start(f32[4,2048]{1,0:T(4,128)S(1)} %broadcast_select_fusion.10), channel_id=1, source_target_pairs={{0,4},{4,8},{8,12},{12,16},{16,20},{20,24},{24,28},{1,5},{5,9},{9,... | collective-permute-start | bytes 98312 | tf_op jit(solution)/shard_map/ppermute | solution.py:15
  62.4 1.1 fusion.15
  63.6 1.2 gather_fusion.9
  64.8 1.5 reshape.260
  66.3 1.8 broadcast_select_fusion.1
  68.1 3.6 %reshape.277 = f32[16,11,64,32]{3,2,1,0:T(8,128)} reshape(f32[16,11,2048]{2,1,0:T(8,128)S(1)} %broadcast_select_fusion.1) | data formatting | bytes 2883584 | tf_op jit(solution)/shard_map/reshape | solution.py:28
  71.7 12.0 %fusion.9 = f32[16,64,32]{1,2,0:T(8,128)S(1)} fusion(f32[16,11,64,64]{3,2,0,1:T(8,128)} %reshape.92, f32[16,11,64,32]{3,2,1,0:T(8,128)} %reshape.277), kind=kOutput, calls=%fused_computation.22 | convolution fusion | flops 276824064 | bytes 4456448 | tf_op jit(solution)/shard_map/fkab,fkbr->far/dot_general | solution.py:29
  86.7 4.0 %collective-permute-start.10 = (f32[4,2048]{1,0:T(4,128)S(1)}, f32[4,2048]{1,0:T(4,128)S(1)}, u32[]{:S(2)}, u32[]{:S(2)}) collective-permute-start(f32[4,2048]{1,0:T(4,128)S(1)} %broadcast_select_fusion.4), channel_id=1, source_target_pairs={{0,1},{1,2},{2,3},{4,5},{5,6},{6,7},{8,9},{9,10},{10,11},{12,13},{... | collective-permute-start | bytes 98312 | tf_op jit(solution)/shard_map/ppermute | solution.py:15
  90.8 1.3 collective-permute-start.11
  92.2 4.8 %collective-permute-start.8 = (f32[4,2048]{1,0:T(4,128)S(1)}, f32[4,2048]{1,0:T(4,128)S(1)}, u32[]{:S(2)}, u32[]{:S(2)}) collective-permute-start(f32[4,2048]{1,0:T(4,128)S(1)} %broadcast_select_fusion.6), channel_id=1, source_target_pairs={{0,4},{4,8},{8,12},{12,16},{16,20},{20,24},{24,28},{1,5},{5,9},{9,... | collective-permute-start | bytes 98312 | tf_op jit(solution)/shard_map/ppermute | solution.py:15
  97.1 1.5 collective-permute-start.9
  98.9 1.3 fusion.39
  100.2 2.8 %collective-permute-done.9 = f32[4,2048]{1,0:T(4,128)S(1)} collective-permute-done((f32[4,2048]{1,0:T(4,128)S(1)}, f32[4,2048]{1,0:T(4,128)S(1)}, u32[]{:S(2)}, u32[]{:S(2)}) %collective-permute-start.9) | collective-permute-done | bytes 32800 | tf_op jit(solution)/shard_map/ppermute | solution.py:15
  103.1 1.2 gather_fusion.14
  104.3 1.6 reshape.272
  105.9 3.2 %broadcast_select_fusion = f32[16,11,2048]{2,1,0:T(8,128)} fusion(f32[16,11,2048]{2,1,0:T(8,128)} %reshape.272, pred[16,11]{1,0:T(8,128)(4,1)S(1)} %compare_and_fusion), kind=kLoop, calls=%fused_computation.25 | loop fusion | flops 360448 | bytes 2883760 | tf_op jit(solution)/shard_map/jit(_take)/select_n | solution.py:65
  109.2 5.2 %reshape.278 = f32[16,11,64,32]{3,2,1,0:T(8,128)} reshape(f32[16,11,2048]{2,1,0:T(8,128)} %broadcast_select_fusion) | data formatting | bytes 2883584 | tf_op jit(solution)/shard_map/reshape | solution.py:28
  114.3 12.0 %fusion.12 = f32[16,64,32]{1,2,0:T(8,128)S(1)} fusion(f32[16,11,64,64]{3,2,0,1:T(8,128)} %reshape.92, f32[16,11,64,32]{3,2,1,0:T(8,128)} %reshape.278), kind=kOutput, calls=%fused_computation.23 | convolution fusion | flops 276824064 | bytes 4456448 | tf_op jit(solution)/shard_map/fkab,fkbr->far/dot_general | solution.py:29
  127.3 1.0 fusion.41
  128.3 48.2 %all-reduce.3 = (f32[96,32]{1,0:T(8,128)S(1)}, f32[64,32]{1,0:T(8,128)S(1)}, f32[32,32]{1,0:T(8,128)S(1)}, f32[128,32]{1,0:T(8,128)S(1)}) all-reduce(f32[96,32]{1,0:T(8,128)S(1)} %fusion.39, f32[64,32]{1,0:T(8,128)S(1)} %fusion.15, f32[32,32]{1,0:T(8,128)S(1)} %fusion.40, ...), channel_id=1, replica_groups=mesh['fx'=8,'fy'=4] {'fx','fy'}, use_global_device_ids=true, to_apply=%region_2.5 | all-reduce | flops 10240 | bytes 81920 | tf_op jit(solution)/shard_map/psum | solution.py:70
  177.7 8.8 %cholesky.16 = f32[96,96]{1,0:T(8,128)S(1)} custom-call(f32[96,96]{1,0:T(8,128)S(1)} %fusion.30), custom_call_target="Cholesky" | custom-call | tf_op jit(solution)/shard_map/jit(cholesky)/cholesky | solution.py:44
  187.2 0.7 fusion.25
  187.8 7.4 %custom-call.10 = f32[1,96,96]{1,2,0:T(8,128)S(1)} custom-call(f32[1,96,96]{2,1,0:T(8,128)S(1)} %fusion.25), custom_call_target="InvertDiagBlocksLowerTriangular" | custom-call | tf_op jit(solution)/shard_map/jit(_cho_solve)/triangular_solve | solution.py:45
  195.9 0.7 fusion.38
  197.2 0.9 reshape.98
  198.1 0.9 reshape.97
  (72 shorter events, 11.7 us)
Async XLA Ops:
  3.1 23.0 %collective-permute-start = (f32[4,2048]{1,0:T(4,128)S(1)}, f32[4,2048]{1,0:T(4,128)S(1)}, u32[]{:S(2)}, u32[]{:S(2)}) collective-permute-start(f32[4,2048]{1,0:T(4,128)S(1)} %broadcast_select_fusion.14), channel_id=1, source_target_pairs={{0,4},{4,8},{8,12},{12,16},{16,20},{20,24},{24,28},{1,5},{5,9},{9,... | collective-permute-start | bytes 98312 | tf_op jit(solution)/shard_map/ppermute | solution.py:15
  9.5 16.5 %collective-permute-start.1 = (f32[4,2048]{1,0:T(4,128)S(1)}, f32[4,2048]{1,0:T(4,128)S(1)}, u32[]{:S(2)}, u32[]{:S(2)}) collective-permute-start(f32[4,2048]{1,0:T(4,128)S(1)} %broadcast_select_fusion.13), channel_id=1, source_target_pairs={{4,0},{8,4},{12,8},{16,12},{20,16},{24,20},{28,24},{5,1},{9,5},{13... | collective-permute-start | bytes 98312 | tf_op jit(solution)/shard_map/ppermute | solution.py:15
  12.4 13.7 %collective-permute-start.2 = (f32[4,2048]{1,0:T(4,128)S(1)}, f32[4,2048]{1,0:T(4,128)S(1)}, u32[]{:S(2)}, u32[]{:S(2)}) collective-permute-start(f32[4,2048]{1,0:T(4,128)S(1)} %broadcast_select_fusion.12), channel_id=1, source_target_pairs={{0,1},{1,2},{2,3},{4,5},{5,6},{6,7},{8,9},{9,10},{10,11},{12,13},{... | collective-permute-start | bytes 98312 | tf_op jit(solution)/shard_map/ppermute | solution.py:15
  15.4 10.6 %collective-permute-start.3 = (f32[4,2048]{1,0:T(4,128)S(1)}, f32[4,2048]{1,0:T(4,128)S(1)}, u32[]{:S(2)}, u32[]{:S(2)}) collective-permute-start(f32[4,2048]{1,0:T(4,128)S(1)} %broadcast_select_fusion.11), channel_id=1, source_target_pairs={{1,0},{2,1},{3,2},{5,4},{6,5},{7,6},{9,8},{10,9},{11,10},{13,12},{... | collective-permute-start | bytes 98312 | tf_op jit(solution)/shard_map/ppermute | solution.py:15
  20.3 5.8 %copy-start = (f32[16,2048]{1,0:T(8,128)S(1)}, f32[16,2048]{1,0:T(8,128)}, u32[]{:S(2)}) copy-start(f32[16,2048]{1,0:T(8,128)} %param.8) | copy-start | bytes 393220
  49.3 14.3 %collective-permute-start.5 = (f32[4,2048]{1,0:T(4,128)S(1)}, f32[4,2048]{1,0:T(4,128)S(1)}, u32[]{:S(2)}, u32[]{:S(2)}) collective-permute-start(f32[4,2048]{1,0:T(4,128)S(1)} %broadcast_select_fusion.9), channel_id=1, source_target_pairs={{4,0},{8,4},{12,8},{16,12},{20,16},{24,20},{28,24},{5,1},{9,5},{13... | collective-permute-start | bytes 98312 | tf_op jit(solution)/shard_map/ppermute | solution.py:15
  50.6 12.9 %collective-permute-start.6 = (f32[4,2048]{1,0:T(4,128)S(1)}, f32[4,2048]{1,0:T(4,128)S(1)}, u32[]{:S(2)}, u32[]{:S(2)}) collective-permute-start(f32[4,2048]{1,0:T(4,128)S(1)} %broadcast_select_fusion.8), channel_id=1, source_target_pairs={{0,1},{1,2},{2,3},{4,5},{5,6},{6,7},{8,9},{9,10},{10,11},{12,13},{... | collective-permute-start | bytes 98312 | tf_op jit(solution)/shard_map/ppermute | solution.py:15
  55.3 8.2 %collective-permute-start.7 = (f32[4,2048]{1,0:T(4,128)S(1)}, f32[4,2048]{1,0:T(4,128)S(1)}, u32[]{:S(2)}, u32[]{:S(2)}) collective-permute-start(f32[4,2048]{1,0:T(4,128)S(1)} %broadcast_select_fusion.7), channel_id=1, source_target_pairs={{1,0},{2,1},{3,2},{5,4},{6,5},{7,6},{9,8},{10,9},{11,10},{13,12},{... | collective-permute-start | bytes 98312 | tf_op jit(solution)/shard_map/ppermute | solution.py:15
  56.7 6.9 %collective-permute-start.4 = (f32[4,2048]{1,0:T(4,128)S(1)}, f32[4,2048]{1,0:T(4,128)S(1)}, u32[]{:S(2)}, u32[]{:S(2)}) collective-permute-start(f32[4,2048]{1,0:T(4,128)S(1)} %broadcast_select_fusion.10), channel_id=1, source_target_pairs={{0,4},{4,8},{8,12},{12,16},{16,20},{20,24},{24,28},{1,5},{5,9},{9,... | collective-permute-start | bytes 98312 | tf_op jit(solution)/shard_map/ppermute | solution.py:15
  86.7 13.5 %collective-permute-start.10 = (f32[4,2048]{1,0:T(4,128)S(1)}, f32[4,2048]{1,0:T(4,128)S(1)}, u32[]{:S(2)}, u32[]{:S(2)}) collective-permute-start(f32[4,2048]{1,0:T(4,128)S(1)} %broadcast_select_fusion.4), channel_id=1, source_target_pairs={{0,1},{1,2},{2,3},{4,5},{5,6},{6,7},{8,9},{9,10},{10,11},{12,13},{... | collective-permute-start | bytes 98312 | tf_op jit(solution)/shard_map/ppermute | solution.py:15
  90.8 9.4 %collective-permute-start.11 = (f32[4,2048]{1,0:T(4,128)S(1)}, f32[4,2048]{1,0:T(4,128)S(1)}, u32[]{:S(2)}, u32[]{:S(2)}) collective-permute-start(f32[4,2048]{1,0:T(4,128)S(1)} %broadcast_select_fusion.3), channel_id=1, source_target_pairs={{1,0},{2,1},{3,2},{5,4},{6,5},{7,6},{9,8},{10,9},{11,10},{13,12},{... | collective-permute-start | bytes 98312 | tf_op jit(solution)/shard_map/ppermute | solution.py:15
  92.2 8.1 %collective-permute-start.8 = (f32[4,2048]{1,0:T(4,128)S(1)}, f32[4,2048]{1,0:T(4,128)S(1)}, u32[]{:S(2)}, u32[]{:S(2)}) collective-permute-start(f32[4,2048]{1,0:T(4,128)S(1)} %broadcast_select_fusion.6), channel_id=1, source_target_pairs={{0,4},{4,8},{8,12},{12,16},{16,20},{20,24},{24,28},{1,5},{5,9},{9,... | collective-permute-start | bytes 98312 | tf_op jit(solution)/shard_map/ppermute | solution.py:15
  97.1 6.0 %collective-permute-start.9 = (f32[4,2048]{1,0:T(4,128)S(1)}, f32[4,2048]{1,0:T(4,128)S(1)}, u32[]{:S(2)}, u32[]{:S(2)}) collective-permute-start(f32[4,2048]{1,0:T(4,128)S(1)} %broadcast_select_fusion.5), channel_id=1, source_target_pairs={{4,0},{8,4},{12,8},{16,12},{20,16},{24,20},{28,24},{5,1},{9,5},{13... | collective-permute-start | bytes 98312 | tf_op jit(solution)/shard_map/ppermute | solution.py:15
where the time goes:
time: 200 us; the launch traced here: 199 us
  blocking collectives  48.2 us (24%)
  matrix products  43.1 us (22%)
  local copies, waits for them, and re-layouts  42.5 us (21%)
  starting transfers between devices  33 us (16%)
  other arithmetic  28.2 us (14%)
  waiting for transfers between devices  2.87 us (1%)
    psum x1, blocking collectives, on_device(): partial_grams.append(lax.psum(local_block, ('fx', 'fy')))  48.2 us
    dot_general x3, matrix products, contract(): jnp.einsum('fkab,fkbr->far', block_mats, shaped, precision=lax.Precision....  36 us
    ppermute x12, starting transfers between devices, from_behind(): return lax.ppermute(block, axis, route)  33 us
    reshape x3, local copies, waits for them, and re-layouts, contract(): shaped = picked.reshape(face_count, picked.shape[1], DOF, NRHS)  12.3 us
    another operation x3, other arithmetic, solve_small(): factor = jnp.linalg.cholesky(normal_matrix)  9.45 us
    gather x6, local copies, waits for them, and re-layouts, on_device(): jnp.take(extended, face_columns, axis=0)  8.18 us
    another operation x2, other arithmetic, solve_small(): coeffs = jax.scipy.linalg.cho_solve((factor, True), right_terms)  8.01 us
    select_n x4, other arithmetic, on_device(): jnp.take(extended, face_columns, axis=0)  7.51 us
  transfers between devices with their start and end apart: 12, of which 1 were waited for; matrix products, arithmetic and copies ran while one was open for 9% of the time, Pallas kernels for 0%

commit v1 on v0

v1 whole, which is shorter than its diff:
```python
import functools

import jax
import jax.numpy as jnp
from jax import lax
from jax.experimental import pallas as pl
from jax.experimental.pallas import tpu as pltpu
from jax.sharding import PartitionSpec as P

DOF = 64
NRHS = 32
BLOCKS = 11
OWNED = 7
POWERS = 3
LANES = 128
HALF = DOF // 2
GROUPS = LANES // NRHS
MESH = pl.DeviceIdType.MESH
f32 = jnp.float32
bf16 = jnp.bfloat16


def split(x):
    hi = x.astype(bf16).astype(f32)
    return hi, x - hi


def lane_group(rows):
    return lax.broadcasted_iota(jnp.int32, (rows, LANES), 1) // NRHS


def pick(group, parts):
    out = parts[-1]
    for index in range(len(parts) - 2, -1, -1):
        out = jnp.where(group == index, parts[index], out)
    return out


def replicate(group, rolled, source):
    return pick(group, [rolled[(lane - source) % GROUPS] for lane in range(GROUPS)])


def rolls(x):
    return [x] + [pltpu.roll(x, step * NRHS, 1) for step in range(1, GROUPS)]


def product_tile(x, group):
    hi, lo = split(x)
    zero = jnp.zeros_like(x)
    top = pick(group, [hi, zero, lo, zero])
    bottom = pick(group, [zero, hi, zero, lo])
    return top.astype(bf16), bottom.astype(bf16)


def kernel(shape, right_ref, coupling_ref, columns_ref, ghost_ref, sol_ref, res_ref,
           stage, spread, mats, w0, w1, w2, w3, tiles, acc, send_buf, recv_buf,
           zbuf, vbuf, gram_buf, plane_recv, line_recv, final_buf, wide,
           load_sem, send_sem, recv_sem, ps_sem, pr_sem, ls_sem, lr_sem, as_sem, ar_sem):
    n_fx, n_fy, low, faces = shape
    plane = low * n_fy
    high = n_fx // low
    i = lax.axis_index("fx")
    j = lax.axis_index("fy")
    my_low = i % low
    my_high = i // low
    my_rank = my_low * n_fy + j
    fields = [w0, w1, w2, w3]

    def plane_target(offset):
        rank = lax.rem(my_rank + offset, plane)
        return rank, (my_high * low + rank // n_fy, rank % n_fy)

    def line_target(offset):
        place = lax.rem(my_high + offset, high)
        return (place * low + my_low, j)

    routes = [
        (1, i < n_fx - 1, (i + 1, j), i > 0),
        (0, i > 0, (i - 1, j), i < n_fx - 1),
        (3, j < n_fy - 1, (i, j + 1), j > 0),
        (2, j > 0, (i, j - 1), j < n_fy - 1),
    ]

    chunk = faces // 4
    loads = [
        pltpu.make_async_copy(
            coupling_ref.at[pl.ds(part * chunk, chunk)], stage.at[pl.ds(part * chunk, chunk)], load_sem.at[part]
        )
        for part in range(4)
    ]
    for load in loads:
        load.start()

    barrier = pltpu.get_barrier_semaphore()
    for _, has_target, target, _ in routes:
        @pl.when(has_target)
        def _(target=target):
            pl.semaphore_signal(barrier, inc=1, device_id=target, device_id_type=MESH)
    for offset in range(1, plane):
        pl.semaphore_signal(barrier, inc=1, device_id=plane_target(offset)[1], device_id_type=MESH)
    for offset in range(1, high):
        pl.semaphore_signal(barrier, inc=1, device_id=line_target(offset), device_id_type=MESH)

    g8 = lane_group(8)
    g64 = lane_group(DOF)
    g32 = lane_group(HALF)

    for block in range(faces // 8):
        for tile in range(DOF // GROUPS):
            x = right_ref[8 * block:8 * block + 8, tile * LANES:(tile + 1) * LANES]
            moved = rolls(x)
            for q in range(GROUPS):
                wide[0, pl.ds(8 * block * DOF + tile * GROUPS + q, 8, stride=DOF), :] = replicate(g8, moved, q)
    for face in range(faces):
        w0[face] = wide[0, face * DOF:(face + 1) * DOF, :]

    def field_copies(power):
        return [
            pltpu.make_async_remote_copy(
                src_ref=send_buf.at[power, q], dst_ref=recv_buf.at[power, q],
                send_sem=send_sem.at[power, q], recv_sem=recv_sem.at[power, q],
                device_id=routes[q][2], device_id_type=MESH,
            )
            for q in range(4)
        ]

    def send_field(power):
        field = fields[power]
        copies = field_copies(power)
        for q, (row, has_target, _, _) in enumerate(routes):
            picked = [field[ghost_ref[row, g]] for g in range(GROUPS)]
            send_buf[power, q] = pick(g64, picked)
        if power == 0:
            count = sum(jnp.where(route[1], 1, 0) for route in routes) + (plane - 1) + (high - 1)
            pl.semaphore_wait(barrier, count)
        for q, (_, has_target, _, _) in enumerate(routes):
            @pl.when(has_target)
            def _(copy=copies[q]):
                copy.start()
        return copies

    def build_own(power):
        field = fields[power]

        @pl.loop(0, faces)
        def _(face):
            x = field[face]
            top, bottom = product_tile(x, g64)
            tiles[face, 0:DOF] = top
            tiles[face, DOF:2 * DOF] = bottom

    def own_products():
        @pl.loop(0, faces // 4)
        def _(quad):
            for sub in range(4):
                face = quad * 4 + sub
                right = jnp.concatenate([tiles[columns_ref[face, k]] for k in range(OWNED)], axis=0)
                out = jnp.dot(mats[face, :, :OWNED * LANES], right, preferred_element_type=f32)
                acc[face] = out[:HALF] + out[HALF:]

    def far_products(power):
        field = fields[power + 1]

        @pl.loop(0, faces // 4)
        def _(quad):
            for sub in range(4):
                face = quad * 4 + sub
                right = jnp.concatenate(
                    [tiles[columns_ref[face, k]] for k in range(OWNED, BLOCKS)], axis=0
                )
                out = jnp.dot(mats[face, :, OWNED * LANES:], right, preferred_element_type=f32)
                total = acc[face] + (out[:HALF] + out[HALF:])
                total = total + pltpu.roll(total, LANES // 2, 1)
                turned = pltpu.roll(total, NRHS, 1)
                even = g32 % 2 == 0
                field[face, pl.ds(0, HALF, stride=2), :] = jnp.where(even, total, turned)
                field[face, pl.ds(1, HALF, stride=2), :] = jnp.where(even, turned, total)

    def receive_field(power, copies):
        for q, (_, has_target, _, has_source) in enumerate(routes):
            @pl.when(has_source)
            def _(copy=copies[q]):
                copy.wait_recv()

            @pl.when(jnp.logical_not(has_source))
            def _(q=q):
                recv_buf[power, q] = jnp.zeros((DOF, LANES), f32)
            moved = rolls(recv_buf[power, q])
            for g in range(GROUPS):
                top, bottom = product_tile(replicate(g64, moved, g), g64)
                tiles[faces + q * GROUPS + g, 0:DOF] = top
                tiles[faces + q * GROUPS + g, DOF:2 * DOF] = bottom

            @pl.when(has_target)
            def _(copy=copies[q]):
                copy.wait_send()

    def prepare():
        for load in loads:
            load.wait()

        @pl.loop(0, faces)
        def _(face):
            for t in range(HALF):
                spread[pl.ds(t, BLOCKS, stride=HALF), :] = stage[face, :, t * LANES:(t + 1) * LANES]
            for k in range(BLOCKS):
                hi, lo = split(spread[k * HALF:(k + 1) * HALF, :])
                mats[face, 0:HALF, k * LANES:(k + 1) * LANES] = hi.astype(bf16)
                mats[face, HALF:DOF, k * LANES:(k + 1) * LANES] = lo.astype(bf16)

    for power in range(POWERS):
        copies = send_field(power)
        build_own(power)
        if power == 0:
            prepare()
        own_products()
        receive_field(power, copies)
        far_products(power)

    @pl.loop(0, faces)
    def _(face):
        rows = pl.ds(pl.multiple_of(face * DOF, DOF), DOF)
        a, b, c, d = [field[face] for field in fields]
        hi, lo = split(pick(g64, [a + b, b + c, c + d, a]))
        zbuf[rows, :LANES] = hi.astype(bf16)
        zbuf[rows, LANES:] = lo.astype(bf16)

    z = zbuf[...]
    both = lax.dot_general(z, z, (((0,), (0,)), ((), ())), preferred_element_type=f32)
    gram = (both[:LANES, :LANES] + both[LANES:, LANES:]) + (both[:LANES, LANES:] + both[LANES:, :LANES])
    share = LANES // plane
    for rank in range(plane):
        gram_buf[rank] = gram[rank * share:(rank + 1) * share]

    copies = []
    for offset in range(1, plane):
        rank, target = plane_target(offset)
        copy = pltpu.make_async_remote_copy(
            src_ref=gram_buf.at[rank], dst_ref=plane_recv.at[offset], send_sem=ps_sem.at[offset],
            recv_sem=pr_sem.at[offset], device_id=target, device_id_type=MESH)
        copy.start()
        copies.append(copy)

    @pl.loop(0, faces)
    def _(face):
        rows = pl.ds(pl.multiple_of(face * DOF, DOF), DOF)
        hi, lo = split(pick(g64, [field[face] for field in fields]))
        vbuf[rows, :LANES] = hi.astype(bf16)
        vbuf[rows, LANES:] = lo.astype(bf16)

    total = gram_buf[my_rank]
    for offset, copy in enumerate(copies, 1):
        copy.wait_recv()
        total = total + plane_recv[offset]
    line_recv[my_high] = total
    line = []
    for offset in range(1, high):
        copy = pltpu.make_async_remote_copy(
            src_ref=line_recv.at[my_high], dst_ref=line_recv.at[my_high], send_sem=ls_sem.at[offset],
            recv_sem=lr_sem.at[offset], device_id=line_target(offset), device_id_type=MESH)
        copy.start()
        line.append(copy)
    for copy in copies:
        copy.wait_send()
    for copy in line:
        copy.wait_recv()
    total = line_recv[0]
    for place in range(1, high):
        total = total + line_recv[place]
    final_buf[my_rank] = total
    gather = []
    for offset in range(1, plane):
        copy = pltpu.make_async_remote_copy(
            src_ref=final_buf.at[my_rank], dst_ref=final_buf.at[my_rank], send_sem=as_sem.at[offset],
            recv_sem=ar_sem.at[offset], device_id=plane_target(offset)[1], device_id_type=MESH)
        copy.start()
        gather.append(copy)
    for copy in line:
        copy.wait_send()
    for copy in gather:
        copy.wait_recv()

    full = jnp.concatenate([final_buf[rank] for rank in range(plane)], axis=0)
    count = POWERS * NRHS
    tiles = [full[8 * t:8 * t + 8] for t in range(count // 8)]
    sub = lax.broadcasted_iota(jnp.int32, (8, LANES), 0)
    for step in range(count):
        home, inner = step // 8, step % 8
        pivot_row = jnp.broadcast_to(tiles[home][inner:inner + 1, :], (8, LANES))
        pivot = jnp.broadcast_to(pivot_row[:, step:step + 1], (8, LANES))
        scaled = pivot_row / pivot
        for t in range(len(tiles)):
            factor = jnp.broadcast_to(tiles[t][:, step:step + 1], (8, LANES))
            new = tiles[t] - factor * scaled
            tiles[t] = jnp.where(sub == inner, scaled, new) if t == home else new
    solved = jnp.concatenate(tiles, axis=0)
    coeffs = replicate(lane_group(count), rolls(solved), GROUPS - 1)
    none = jnp.zeros((NRHS, LANES), f32)
    row = lax.broadcasted_iota(jnp.int32, (LANES, LANES), 0)
    col = lax.broadcasted_iota(jnp.int32, (LANES, LANES), 1) % NRHS
    first = jnp.where(row == col, 1.0, 0.0)
    padded = jnp.concatenate([coeffs, none], axis=0)
    combo = first - (padded + jnp.concatenate([none, coeffs], axis=0))
    hi, lo = split(jnp.concatenate([padded, combo], axis=1))
    hi, lo = hi.astype(bf16), lo.astype(bf16)
    twice = jnp.concatenate([hi, hi], axis=0)

    @pl.loop(0, faces // 4)
    def _(quad):
        rows = pl.ds(pl.multiple_of(quad * 4 * DOF, 4 * DOF), 4 * DOF)
        left = vbuf[rows, :]
        out = jnp.dot(left, twice, preferred_element_type=f32)
        wide_part = out + jnp.dot(left[:, :LANES], lo, preferred_element_type=f32)
        wide[0, rows, :] = wide_part[:, :LANES]
        wide[1, rows, :] = wide_part[:, LANES:]
    for part, out_ref in enumerate((sol_ref, res_ref)):
        for block in range(faces // 8):
            for tile in range(DOF // GROUPS):
                parts = [
                    wide[part, pl.ds(8 * block * DOF + tile * GROUPS + q, 8, stride=DOF), :] for q in range(GROUPS)
                ]
                out_ref[8 * block:8 * block + 8, tile * LANES:(tile + 1) * LANES] = pick(g8, parts)
    for copy in gather:
        copy.wait_send()


def on_device(shape, right_side, coupling, face_columns, ghost_lists):
    n_fx, n_fy, low, faces = shape
    plane = low * n_fy
    high = n_fx // low
    share = LANES // plane
    rows = faces * DOF
    vmem = pl.BlockSpec(memory_space=pltpu.VMEM)
    smem = pl.BlockSpec(memory_space=pltpu.SMEM)
    dma = pltpu.SemaphoreType.DMA
    out = jax.ShapeDtypeStruct(right_side.shape, f32)
    return pl.pallas_call(
        functools.partial(kernel, shape),
        out_shape=(out, out),
        in_specs=[vmem, pl.BlockSpec(memory_space=pl.ANY), smem, smem],
        out_specs=(vmem, vmem),
        scratch_shapes=[
            pltpu.VMEM(coupling.shape, f32),
            pltpu.VMEM((BLOCKS * HALF, LANES), f32),
            pltpu.VMEM((faces, DOF, BLOCKS * LANES), bf16),
        ]
        + [pltpu.VMEM((faces, DOF, LANES), f32)] * (POWERS + 1)
        + [
            pltpu.VMEM((faces + 4 * GROUPS, LANES, LANES), bf16),
            pltpu.VMEM((faces, HALF, LANES), f32),
            pltpu.VMEM((POWERS, 4, DOF, LANES), f32),
            pltpu.VMEM((POWERS, 4, DOF, LANES), f32),
            pltpu.VMEM((rows, 2 * LANES), bf16),
            pltpu.VMEM((rows, 2 * LANES), bf16),
            pltpu.VMEM((plane, share, LANES), f32),
            pltpu.VMEM((plane, share, LANES), f32),
            pltpu.VMEM((high, share, LANES), f32),
            pltpu.VMEM((plane, share, LANES), f32),
            pltpu.VMEM((2, rows, LANES), f32),
            dma((4,)),
            dma((POWERS, 4)),
            dma((POWERS, 4)),
            dma((plane,)),
            dma((plane,)),
            dma((high,)),
            dma((high,)),
            dma((plane,)),
            dma((plane,)),
        ],
        compiler_params=pltpu.CompilerParams(
            collective_id=0, has_side_effects=True, vmem_limit_bytes=40 * 2**20
        ),
    )(right_side, coupling, face_columns, ghost_lists)


def solution(mesh):
    n_fx, n_fy = mesh.shape["fx"], mesh.shape["fy"]
    low = 1
    while low * low * 4 <= n_fx:
        low *= 2

    def body(right_side, coupling, face_columns, ghost_lists):
        shape = (n_fx, n_fy, low, right_side.shape[0])
        return on_device(shape, right_side, coupling, face_columns, ghost_lists)

    placed = (
        P(("fx", "fy"), None),
        P(("fx", "fy"), None, None),
        P(("fx", "fy"), None),
        P(("fx", "fy"), None),
    )
    return jax.shard_map(
        body,
        mesh=mesh,
        in_specs=placed,
        out_specs=(P(("fx", "fy"), None), P(("fx", "fy"), None)),
        check_vma=False,
    )
```

time: 200 us -> 54.9 us (0.27)
  Pallas kernels: 0 us -> 49.2 us
  blocking collectives: 48.2 us -> 0 us
  matrix products: 43.1 us -> 0 us
  local copies, waits for them, and re-layouts: 42.5 us -> 4.91 us
  starting transfers between devices: 33 us -> 0 us
  other arithmetic: 28.2 us -> 0 us
  waiting for transfers between devices: 2.87 us -> 0 us
    pallas_call x0 -> x1, Pallas kernels: none -> 49.2 us  [on_device(): pl.pallas_call(functools.partial(kernel, shape), out_shape=(out, out), in...]
    psum x1 -> x0, blocking collectives: 48.2 us -> none  [on_device(): partial_grams.append(lax.psum(local_block, ('fx', 'fy')))]
    dot_general x13 -> x0, matrix products: 42.6 us -> none  [the longest x3 36 us: contract(): jnp.einsum('fkab,fkbr->far', block_mats, shaped, precision=lax.Precision....]
    ppermute x12 -> x0, starting transfers between devices: 33 us -> none  [from_behind(): return lax.ppermute(block, axis, route)]
    reshape x9 -> x0, local copies, waits for them, and re-layouts: 21.4 us -> none  [the longest x3 12.3 us: contract(): shaped = picked.reshape(face_count, picked.shape[1], DOF, NRHS)]
    gather x18 -> x0, local copies, waits for them, and re-layouts: 18.7 us -> none  [the longest x6 8.18 us: on_device(): jnp.take(extended, face_columns, axis=0)]
    another operation x5 -> x0, other arithmetic: 17.5 us -> none  [the longest x3 9.45 us: solve_small(): factor = jnp.linalg.cholesky(normal_matrix)]
    select_n x18 -> x0, other arithmetic: 8.56 us -> none  [the longest x4 7.51 us: on_device(): jnp.take(extended, face_columns, axis=0)]
  transfers between devices with their start and end apart: 12 -> 0, of which waited for: 1 -> 0; matrix products, arithmetic and copies ran while one was open for 9% -> 0% of each run, Pallas kernels for 0% -> 0%
where the time goes in v1:
time: 54.9 us; the launch traced here: 54.8 us
  Pallas kernels  49.2 us (90%)
  local copies, waits for them, and re-layouts  4.91 us (9%)
  between operations  0.69 us (1%)
    pallas_call x1, Pallas kernels, on_device(): pl.pallas_call(functools.partial(kernel, shape), out_shape=(out, out), in...  49.2 us
    unnamed x9, local copies, waits for them, and re-layouts  4.91 us

profile of v1, /device:TPU:0, one launch (start us, length us, event | category | flops | bytes accessed | tf_op | source)
XLA Modules:
  0.0 54.8 jit_solution(14665166552837342082)
XLA Ops:
  0.6 0.0 copy-start.2
  0.6 0.0 copy-start.1
  0.7 0.0 copy-start
  0.7 3.6 %copy.6.coupling_ref = f32[16,11,4096]{2,1,0:T(8,128)S(1)} copy(f32[16,11,4096]{2,0,1:T(8,128)} %param.5) | data formatting | bytes 5767168 | tf_op args[1]
  4.3 0.0 copy-done.2
  4.3 0.0 copy-done.1
  4.3 0.0 copy-done
  4.3 49.2 %shard_map.59 = (f32[16,2048]{1,0:T(8,128)S(1)}, f32[16,2048]{1,0:T(8,128)S(1)}) custom-call(f32[16,2048]{1,0:T(8,128)S(1)} %copy-done, f32[16,11,4096]{2,1,0:T(8,128)S(1)} %copy.6.coupling_ref, s32[16,11]{1,0:T(8,128)S(1)} %copy-done.1, s32[4,4]{1,0:T(4,128)S(1)} %copy-done.2), custom_call_target="tpu_custom_call" | custom-call | tf_op jit(solution)/shard_map/pallas_call | solution.py:337
  53.5 0.7 %copy.9 = f32[16,2048]{1,0:T(8,128)} copy(f32[16,2048]{1,0:T(8,128)S(1)} %get-tuple-element.4) | data formatting | bytes 262144
  54.1 0.7 %copy.10 = f32[16,2048]{1,0:T(8,128)} copy(f32[16,2048]{1,0:T(8,128)S(1)} %get-tuple-element.5) | data formatting | bytes 262144
Async XLA Ops:
  0.6 3.6 %copy-start.2 = (s32[4,4]{1,0:T(4,128)S(1)}, s32[4,4]{1,0:T(4,128)}, u32[]{:S(2)}) copy-start(s32[4,4]{1,0:T(4,128)} %ghost_ref.1) | copy-start | bytes 196
  0.6 3.6 %copy-start.1 = (s32[16,11]{1,0:T(8,128)S(1)}, s32[16,11]{1,0:T(8,128)}, u32[]{:S(2)}) copy-start(s32[16,11]{1,0:T(8,128)} %columns_ref.1) | copy-start | bytes 2116
  0.7 3.6 %copy-start = (f32[16,2048]{1,0:T(8,128)S(1)}, f32[16,2048]{1,0:T(8,128)}, u32[]{:S(2)}) copy-start(f32[16,2048]{1,0:T(8,128)} %right_ref.1) | copy-start | bytes 393220

commit v2 on v1

--- a/solution.py
+++ b/solution.py
@@ -14,6 +14,7 @@
 POWERS = 3
 LANES = 128
 HALF = DOF // 2
+UNROLL = 16
 GROUPS = LANES // NRHS
 MESH = pl.DeviceIdType.MESH
 f32 = jnp.float32
@@ -81,13 +82,7 @@
         (2, j > 0, (i, j - 1), j < n_fy - 1),
     ]
 
-    chunk = faces // 4
-    loads = [
-        pltpu.make_async_copy(
-            coupling_ref.at[pl.ds(part * chunk, chunk)], stage.at[pl.ds(part * chunk, chunk)], load_sem.at[part]
-        )
-        for part in range(4)
-    ]
+    loads = [pltpu.make_async_copy(coupling_ref.at[k], stage.at[k], load_sem.at[k]) for k in range(BLOCKS)]
     for load in loads:
         load.start()
 
@@ -150,10 +145,10 @@
             tiles[face, DOF:2 * DOF] = bottom
 
     def own_products():
-        @pl.loop(0, faces // 4)
-        def _(quad):
-            for sub in range(4):
-                face = quad * 4 + sub
+        @pl.loop(0, faces // UNROLL)
+        def _(part):
+            for sub in range(UNROLL):
+                face = part * UNROLL + sub
                 right = jnp.concatenate([tiles[columns_ref[face, k]] for k in range(OWNED)], axis=0)
                 out = jnp.dot(mats[face, :, :OWNED * LANES], right, preferred_element_type=f32)
                 acc[face] = out[:HALF] + out[HALF:]
@@ -161,10 +156,10 @@
     def far_products(power):
         field = fields[power + 1]
 
-        @pl.loop(0, faces // 4)
-        def _(quad):
-            for sub in range(4):
-                face = quad * 4 + sub
+        @pl.loop(0, faces // UNROLL)
+        def _(part):
+            for sub in range(UNROLL):
+                face = part * UNROLL + sub
                 right = jnp.concatenate(
                     [tiles[columns_ref[face, k]] for k in range(OWNED, BLOCKS)], axis=0
                 )
@@ -196,15 +191,14 @@
                 copy.wait_send()
 
     def prepare():
-        for load in loads:
-            load.wait()
-
-        @pl.loop(0, faces)
-        def _(face):
-            for t in range(HALF):
-                spread[pl.ds(t, BLOCKS, stride=HALF), :] = stage[face, :, t * LANES:(t + 1) * LANES]
-            for k in range(BLOCKS):
-                hi, lo = split(spread[k * HALF:(k + 1) * HALF, :])
+        for k in range(BLOCKS):
+            loads[k].wait()
+            for block in range(faces // 8):
+                for t in range(HALF):
+                    spread[k % 2, pl.ds(8 * block * HALF + t, 8, stride=HALF), :] = stage[
+                        k, 8 * block:8 * block + 8, t * LANES:(t + 1) * LANES]
+            for face in range(faces):
+                hi, lo = split(spread[k % 2, face * HALF:(face + 1) * HALF, :])
                 mats[face, 0:HALF, k * LANES:(k + 1) * LANES] = hi.astype(bf16)
                 mats[face, HALF:DOF, k * LANES:(k + 1) * LANES] = lo.astype(bf16)
 
@@ -284,15 +278,33 @@
     count = POWERS * NRHS
     tiles = [full[8 * t:8 * t + 8] for t in range(count // 8)]
     sub = lax.broadcasted_iota(jnp.int32, (8, LANES), 0)
-    for step in range(count):
-        home, inner = step // 8, step % 8
-        pivot_row = jnp.broadcast_to(tiles[home][inner:inner + 1, :], (8, LANES))
-        pivot = jnp.broadcast_to(pivot_row[:, step:step + 1], (8, LANES))
-        scaled = pivot_row / pivot
-        for t in range(len(tiles)):
-            factor = jnp.broadcast_to(tiles[t][:, step:step + 1], (8, LANES))
-            new = tiles[t] - factor * scaled
-            tiles[t] = jnp.where(sub == inner, scaled, new) if t == home else new
+
+    def across(x, lane):
+        return jnp.broadcast_to(x[:, lane:lane + 1], (8, LANES))
+
+    def down(x, row):
+        return jnp.broadcast_to(x[row:row + 1, :], (8, LANES))
+
+    for home in range(len(tiles)):
+        mine = tiles[home]
+        cols = [across(mine, 8 * home + c) for c in range(8)]
+        for step in range(8):
+            inverse = 1.0 / down(cols[step], step)
+            here = sub == step
+            factor = cols[step]
+            scaled = down(mine, step) * inverse
+            mine = jnp.where(here, scaled, mine - factor * scaled)
+            for c in range(step + 1, 8):
+                scaled = down(cols[c], step) * inverse
+                cols[c] = jnp.where(here, scaled, cols[c] - factor * scaled)
+        tiles[home] = mine
+        rows8 = [down(mine, c) for c in range(8)]
+        order = [t % len(tiles) for t in range(home + 1, home + len(tiles))]
+        for t in order:
+            terms = [across(tiles[t], 8 * home + c) * rows8[c] for c in range(8)]
+            while len(terms) > 1:
+                terms = [terms[k] + terms[k + 1] for k in range(0, len(terms), 2)]
+            tiles[t] = tiles[t] - terms[0]
     solved = jnp.concatenate(tiles, axis=0)
     coeffs = replicate(lane_group(count), rolls(solved), GROUPS - 1)
     none = jnp.zeros((NRHS, LANES), f32)
@@ -337,11 +349,11 @@
     return pl.pallas_call(
         functools.partial(kernel, shape),
         out_shape=(out, out),
-        in_specs=[vmem, pl.BlockSpec(memory_space=pl.ANY), smem, smem],
+        in_specs=[vmem, pl.BlockSpec(memory_space=pltpu.HBM), smem, smem],
         out_specs=(vmem, vmem),
         scratch_shapes=[
             pltpu.VMEM(coupling.shape, f32),
-            pltpu.VMEM((BLOCKS * HALF, LANES), f32),
+            pltpu.VMEM((2, faces * HALF, LANES), f32),
             pltpu.VMEM((faces, DOF, BLOCKS * LANES), bf16),
         ]
         + [pltpu.VMEM((faces, DOF, LANES), f32)] * (POWERS + 1)
@@ -357,7 +369,7 @@
             pltpu.VMEM((high, share, LANES), f32),
             pltpu.VMEM((plane, share, LANES), f32),
             pltpu.VMEM((2, rows, LANES), f32),
-            dma((4,)),
+            dma((BLOCKS,)),
             dma((POWERS, 4)),
             dma((POWERS, 4)),
             dma((plane,)),
@@ -368,7 +380,7 @@
             dma((plane,)),
         ],
         compiler_params=pltpu.CompilerParams(
-            collective_id=0, has_side_effects=True, vmem_limit_bytes=40 * 2**20
+            collective_id=0, has_side_effects=True, vmem_limit_bytes=62 * 2**20
         ),
     )(right_side, coupling, face_columns, ghost_lists)
 
@@ -381,7 +393,7 @@
 
     def body(right_side, coupling, face_columns, ghost_lists):
         shape = (n_fx, n_fy, low, right_side.shape[0])
-        return on_device(shape, right_side, coupling, face_columns, ghost_lists)
+        return on_device(shape, right_side, coupling.transpose(1, 0, 2), face_columns, ghost_lists)
 
     placed = (
         P(("fx", "fy"), None),

time: 54.9 us -> 40.2 us (0.73)
  Pallas kernels: 49.2 us -> 36.3 us
  local copies, waits for them, and re-layouts: 4.91 us -> 3.14 us
    pallas_call x1, Pallas kernels: 49.2 us -> 36.3 us  [on_device(): pl.pallas_call(functools.partial(kernel, shape), out_shape=(out, out), in...]
    unnamed x9 -> x2, local copies, waits for them, and re-layouts: 4.91 us -> 3.14 us
where the time goes in v2:
time: 40.2 us; the launch traced here: 40 us
  Pallas kernels  36.3 us (90%)
  local copies, waits for them, and re-layouts  3.14 us (8%)
  between operations  0.64 us (2%)
    pallas_call x1, Pallas kernels, on_device(): pl.pallas_call(functools.partial(kernel, shape), out_shape=(out, out), in...  36.3 us
    unnamed x2, local copies, waits for them, and re-layouts  3.14 us

profile of v2, /device:TPU:0, one launch (start us, length us, event | category | flops | bytes accessed | tf_op | source)
XLA Modules:
  0.0 40.0 jit_solution(1029195678703691416)
XLA Ops:
  0.6 36.3 %shard_map.59 = (f32[16,2048]{1,0:T(8,128)}, f32[16,2048]{1,0:T(8,128)}) custom-call(f32[16,2048]{1,0:T(8,128)} %right_ref.1, f32[11,16,4096]{2,1,0:T(8,128)} %bitcast.1, s32[16,11]{1,0:T(8,128)} %columns_ref.1, s32[4,4]{1,0:T(4,128)} %ghost_ref.1), custom_call_target="tpu_custom_call" | custom-call | tf_op jit(solution)/shard_map/pallas_call | solution.py:349
  36.9 1.6 %copy.8 = f32[16,2048]{1,0:T(8,128)} copy(f32[16,2048]{1,0:T(8,128)} %get-tuple-element.4) | data formatting | bytes 262144
  38.5 1.6 %copy.9 = f32[16,2048]{1,0:T(8,128)} copy(f32[16,2048]{1,0:T(8,128)} %get-tuple-element.5) | data formatting | bytes 262144

commit v3 on v2

--- a/solution.py
+++ b/solution.py
@@ -172,7 +172,9 @@
                 field[face, pl.ds(1, HALF, stride=2), :] = jnp.where(even, turned, total)
 
     def receive_field(power, copies):
-        for q, (_, has_target, _, has_source) in enumerate(routes):
+        for q in (2, 3, 0, 1):
+            _, has_target, _, has_source = routes[q]
+
             @pl.when(has_source)
             def _(copy=copies[q]):
                 copy.wait_recv()
@@ -380,9 +382,9 @@
             dma((plane,)),
         ],
         compiler_params=pltpu.CompilerParams(
-            collective_id=0, has_side_effects=True, vmem_limit_bytes=62 * 2**20
+            collective_id=0, has_side_effects=True, vmem_limit_bytes=40 * 2**20
         ),
-    )(right_side, coupling, face_columns, ghost_lists)
+    )(right_side, pltpu.with_memory_space_constraint(coupling, pltpu.HBM), face_columns, ghost_lists)
 
 
 def solution(mesh):

time: 40.2 us -> 39 us (0.970)
  Pallas kernels: 36.3 us -> 34.6 us
  local copies, waits for them, and re-layouts: 3.14 us -> 3.59 us
    pallas_call x1, Pallas kernels: 36.3 us -> 34.6 us  [on_device(): pl.pallas_call(functools.partial(kernel, shape), out_shape=(out, out), in...]
    unnamed x2 -> x8, local copies, waits for them, and re-layouts: 3.14 us -> 3.59 us
where the time goes in v3:
time: 39 us; the launch traced here: 38.8 us
  Pallas kernels  34.6 us (89%)
  local copies, waits for them, and re-layouts  3.59 us (9%)
  between operations  0.65 us (2%)
    pallas_call x1, Pallas kernels, on_device(): pl.pallas_call(functools.partial(kernel, shape), out_shape=(out, out), in...  34.6 us
    unnamed x8, local copies, waits for them, and re-layouts  3.59 us

profile of v3, /device:TPU:0, one launch (start us, length us, event | category | flops | bytes accessed | tf_op | source)
XLA Modules:
  0.0 38.8 jit_solution(15453515108706256165)
XLA Ops:
  0.6 0.0 copy-start
  0.6 0.9 %copy-done = f32[16,2048]{1,0:T(8,128)S(1)} copy-done((f32[16,2048]{1,0:T(8,128)S(1)}, f32[16,2048]{1,0:T(8,128)}, u32[]{:S(2)}) %copy-start) | copy-done | bytes 131096
  1.5 0.0 copy-start.1
  1.5 0.7 %copy-done.1 = s32[16,11]{1,0:T(8,128)S(1)} copy-done((s32[16,11]{1,0:T(8,128)S(1)}, s32[16,11]{1,0:T(8,128)}, u32[]{:S(2)}) %copy-start.1) | copy-done | bytes 728
  2.2 0.0 copy-start.2
  2.2 0.7 %copy-done.2 = s32[4,4]{1,0:T(4,128)S(1)} copy-done((s32[4,4]{1,0:T(4,128)S(1)}, s32[4,4]{1,0:T(4,128)}, u32[]{:S(2)}) %copy-start.2) | copy-done | bytes 88
  2.9 34.6 %shard_map.59 = (f32[16,2048]{1,0:T(8,128)S(1)}, f32[16,2048]{1,0:T(8,128)S(1)}) custom-call(f32[16,2048]{1,0:T(8,128)S(1)} %copy-done, f32[11,16,4096]{2,1,0:T(8,128)} %bitcast.1, s32[16,11]{1,0:T(8,128)S(1)} %copy-done.1, s32[4,4]{1,0:T(4,128)S(1)} %copy-done.2), custom_call_target="tpu_custom_call" | custom-call | tf_op jit(solution)/shard_map/pallas_call | solution.py:351
  37.5 0.7 %copy.8 = f32[16,2048]{1,0:T(8,128)} copy(f32[16,2048]{1,0:T(8,128)S(1)} %get-tuple-element.4) | data formatting | bytes 262144
  38.2 0.7 %copy.9 = f32[16,2048]{1,0:T(8,128)} copy(f32[16,2048]{1,0:T(8,128)S(1)} %get-tuple-element.5) | data formatting | bytes 262144
Async XLA Ops:
  0.6 0.9 %copy-start = (f32[16,2048]{1,0:T(8,128)S(1)}, f32[16,2048]{1,0:T(8,128)}, u32[]{:S(2)}) copy-start(f32[16,2048]{1,0:T(8,128)} %right_ref.1) | copy-start | bytes 393220
  1.5 0.7 %copy-start.1 = (s32[16,11]{1,0:T(8,128)S(1)}, s32[16,11]{1,0:T(8,128)}, u32[]{:S(2)}) copy-start(s32[16,11]{1,0:T(8,128)} %columns_ref.1) | copy-start | bytes 2116
  2.2 0.7 %copy-start.2 = (s32[4,4]{1,0:T(4,128)S(1)}, s32[4,4]{1,0:T(4,128)}, u32[]{:S(2)}) copy-start(s32[4,4]{1,0:T(4,128)} %ghost_ref.1) | copy-start | bytes 196

commit v4 on v3

--- a/solution.py
+++ b/solution.py
@@ -125,10 +125,10 @@
         for q, (row, has_target, _, _) in enumerate(routes):
             picked = [field[ghost_ref[row, g]] for g in range(GROUPS)]
             send_buf[power, q] = pick(g64, picked)
-        if power == 0:
-            count = sum(jnp.where(route[1], 1, 0) for route in routes) + (plane - 1) + (high - 1)
-            pl.semaphore_wait(barrier, count)
-        for q, (_, has_target, _, _) in enumerate(routes):
+            if power == 0 and q == 0:
+                count = sum(jnp.where(route[1], 1, 0) for route in routes) + (plane - 1) + (high - 1)
+                pl.semaphore_wait(barrier, count)
+
             @pl.when(has_target)
             def _(copy=copies[q]):
                 copy.start()
@@ -137,7 +137,7 @@
     def build_own(power):
         field = fields[power]
 
-        @pl.loop(0, faces)
+        @pl.loop(0, faces, unroll=4)
         def _(face):
             x = field[face]
             top, bottom = product_tile(x, g64)
@@ -213,7 +213,7 @@
         receive_field(power, copies)
         far_products(power)
 
-    @pl.loop(0, faces)
+    @pl.loop(0, faces, unroll=4)
     def _(face):
         rows = pl.ds(pl.multiple_of(face * DOF, DOF), DOF)
         a, b, c, d = [field[face] for field in fields]
@@ -237,7 +237,7 @@
         copy.start()
         copies.append(copy)
 
-    @pl.loop(0, faces)
+    @pl.loop(0, faces, unroll=4)
     def _(face):
         rows = pl.ds(pl.multiple_of(face * DOF, DOF), DOF)
         hi, lo = split(pick(g64, [field[face] for field in fields]))
@@ -319,7 +319,7 @@
     hi, lo = hi.astype(bf16), lo.astype(bf16)
     twice = jnp.concatenate([hi, hi], axis=0)
 
-    @pl.loop(0, faces // 4)
+    @pl.loop(0, faces // 4, unroll=True)
     def _(quad):
         rows = pl.ds(pl.multiple_of(quad * 4 * DOF, 4 * DOF), 4 * DOF)
         left = vbuf[rows, :]

time: 39 us -> 38.7 us (level)
  no operation moved by 1% of the time
where the time goes in v4:
time: 38.7 us; the launch traced here: 38.5 us
  Pallas kernels  34.3 us (89%)
  local copies, waits for them, and re-layouts  3.59 us (9%)
  between operations  0.65 us (2%)
    pallas_call x1, Pallas kernels, on_device(): pl.pallas_call(functools.partial(kernel, shape), out_shape=(out, out), in...  34.3 us
    unnamed x8, local copies, waits for them, and re-layouts  3.59 us

profile of v4, /device:TPU:0, one launch (start us, length us, event | category | flops | bytes accessed | tf_op | source)
XLA Modules:
  0.0 38.5 jit_solution(14966912380122649099)
XLA Ops:
  0.6 0.0 copy-start
  0.6 0.9 %copy-done = f32[16,2048]{1,0:T(8,128)S(1)} copy-done((f32[16,2048]{1,0:T(8,128)S(1)}, f32[16,2048]{1,0:T(8,128)}, u32[]{:S(2)}) %copy-start) | copy-done | bytes 131096
  1.5 0.0 copy-start.1
  1.5 0.7 %copy-done.1 = s32[16,11]{1,0:T(8,128)S(1)} copy-done((s32[16,11]{1,0:T(8,128)S(1)}, s32[16,11]{1,0:T(8,128)}, u32[]{:S(2)}) %copy-start.1) | copy-done | bytes 728
  2.2 0.0 copy-start.2
  2.2 0.7 %copy-done.2 = s32[4,4]{1,0:T(4,128)S(1)} copy-done((s32[4,4]{1,0:T(4,128)S(1)}, s32[4,4]{1,0:T(4,128)}, u32[]{:S(2)}) %copy-start.2) | copy-done | bytes 88
  2.9 34.3 %shard_map.59 = (f32[16,2048]{1,0:T(8,128)S(1)}, f32[16,2048]{1,0:T(8,128)S(1)}) custom-call(f32[16,2048]{1,0:T(8,128)S(1)} %copy-done, f32[11,16,4096]{2,1,0:T(8,128)} %bitcast.1, s32[16,11]{1,0:T(8,128)S(1)} %copy-done.1, s32[4,4]{1,0:T(4,128)S(1)} %copy-done.2), custom_call_target="tpu_custom_call" | custom-call | tf_op jit(solution)/shard_map/pallas_call | solution.py:351
  37.2 0.7 %copy.8 = f32[16,2048]{1,0:T(8,128)} copy(f32[16,2048]{1,0:T(8,128)S(1)} %get-tuple-element.4) | data formatting | bytes 262144
  37.8 0.7 %copy.9 = f32[16,2048]{1,0:T(8,128)} copy(f32[16,2048]{1,0:T(8,128)S(1)} %get-tuple-element.5) | data formatting | bytes 262144
Async XLA Ops:
  0.6 0.9 %copy-start = (f32[16,2048]{1,0:T(8,128)S(1)}, f32[16,2048]{1,0:T(8,128)}, u32[]{:S(2)}) copy-start(f32[16,2048]{1,0:T(8,128)} %right_ref.1) | copy-start | bytes 393220
  1.5 0.7 %copy-start.1 = (s32[16,11]{1,0:T(8,128)S(1)}, s32[16,11]{1,0:T(8,128)}, u32[]{:S(2)}) copy-start(s32[16,11]{1,0:T(8,128)} %columns_ref.1) | copy-start | bytes 2116
  2.2 0.7 %copy-start.2 = (s32[4,4]{1,0:T(4,128)S(1)}, s32[4,4]{1,0:T(4,128)}, u32[]{:S(2)}) copy-start(s32[4,4]{1,0:T(4,128)} %ghost_ref.1) | copy-start | bytes 196
